TPU v7x, 32 devices: a whole 2x2x4 slice. The times are simulated.
32 devices in a mesh: grp: 1, ev: 32 (over z, y, x, core).
Axes of the slice: x: 2, y: 2, z: 4, core: 2. Of those that a mesh axis runs over, the one named last changes fastest.
Arguments:
- windows: bfloat16 [256, 3, 64, 1024], P(('grp', 'ev')), may hold values from -400 to 400, as said below
- rotation: bfloat16 [256, 3, 64], P(('grp', 'ev')), may hold values from -3 to 3
- source_inverse: bfloat16 [256, 1024], P(('grp', 'ev')), may hold values from -3.4 to 3.4
- send_rows: int32 [1024, 64], P(('grp', 'ev')), may hold values from 0 to 511, as said below
- tile_station: int32 [2048], P(('grp', 'ev')), may hold values from 0 to 63, as said below
- tile_count: int32 [2048], P(('grp', 'ev')), may hold values from 16 to 128
- pair_rows: int32 [2, 262144], P(None, ('grp', 'ev')), may hold values from 0 to 2047, as said below
Outputs:
- correlation: float32 [262144, 255], P(('grp', 'ev'))
Inputs may be any that keep to these rules, and one draw needn't show every extreme that they name: Each event's windows carry a scale of their own, and each station's another. `send_rows`: row j of the block of device o names the rows of device o sent to device j, each as local event times 64 plus station, with the station of the tile whose residue matches the receiving slot (o * 64 + k) mod 64. `tile_station`: tile t of a device is fed by received slots r with r mod 64 = t mod 64, all at the tile's station. `pair_rows`: entries count the rows a device receives by sending device then slot; both members of a slot lie at its tile's station.
All inputs are finite; a program needn't handle non-finite values.
Results may differ from a plain program's by a relative error of at most 0.007.
Values may be sent and summed in bfloat16 or wider, within the bound.
No kernel may reach another device: no remote copies, remote signals or barrier semaphores. Data moves between devices by JAX's collectives and lax.ppermute only.
A program may use at most 64 MiB of HBM per device.

v0:
```python
from functools import partial
import math
import jax
import jax.numpy as jnp
from jax import lax
from jax.sharding import PartitionSpec as P

LAGS = 255
epsilon = 1e-06


def spectral_table(length):
    half_len = length // 2
    samples = jnp.arange(length, dtype=jnp.int32)[:, None]
    frequency = jnp.arange(half_len, dtype=jnp.int32)[None, :]
    angles = (samples * frequency % length).astype(jnp.float32) * (2.0 * math.pi / length)
    factor = 1.0 / math.sqrt(length)
    return jnp.concatenate([jnp.cos(angles) * factor, -jnp.sin(angles) * factor], axis=1).astype(
        jnp.bfloat16
    )


def lag_table(length, lag_count):
    half_len = length // 2
    frequency = jnp.arange(half_len, dtype=jnp.int32)[:, None]
    shifts = jnp.arange(lag_count, dtype=jnp.int32)[None, :] - lag_count // 2
    angles = (frequency * shifts % length).astype(jnp.float32) * (2.0 * math.pi / length)
    factor = 1.0 / math.sqrt(half_len)
    return jnp.concatenate([jnp.cos(angles) * factor, -jnp.sin(angles) * factor], axis=0).astype(
        jnp.bfloat16
    )


def event_spectra(windows, rotation, source_inverse, dft_table):
    half_len = dft_table.shape[1] // 2
    transverse = jnp.sum(
        rotation.astype(jnp.float32)[..., None] * windows.astype(jnp.float32), axis=1
    ).astype(jnp.bfloat16)
    events, stations, length = transverse.shape
    spectrum = jnp.dot(
        transverse.reshape(events * stations, length), dft_table, preferred_element_type=jnp.float32
    )
    spectrum = spectrum.reshape(events, stations, length)
    filter_gain = source_inverse.astype(jnp.float32)[:, None, :]
    real_in, imag_in = (spectrum[..., :half_len], spectrum[..., half_len:])
    real_gain, imag_gain = (filter_gain[..., :half_len], filter_gain[..., half_len:])
    return jnp.concatenate(
        [real_in * real_gain - imag_in * imag_gain, real_in * imag_gain + imag_in * real_gain],
        axis=-1,
    )


def correlate_group(spectra, lag_tab, tile_pairs, pieces):
    first_rows, second_rows, weights, counts = pieces
    half_len = spectra.shape[1] // 2
    first_spec = spectra[first_rows].astype(jnp.float32)
    second_spec = spectra[second_rows].astype(jnp.float32)
    first_re, first_im = (first_spec[:, :half_len], first_spec[:, half_len:])
    second_re, second_im = (second_spec[:, :half_len], second_spec[:, half_len:])
    row_weight = jnp.repeat(weights, tile_pairs, axis=0)
    cross_spec = jnp.concatenate(
        [
            (first_re * second_re + first_im * second_im) * row_weight,
            (first_im * second_re - first_re * second_im) * row_weight,
        ],
        axis=1,
    ).astype(jnp.bfloat16)
    lagged = jnp.dot(cross_spec, lag_tab, preferred_element_type=jnp.float32)
    live_rows = jnp.arange(lagged.shape[0], dtype=jnp.int32) % tile_pairs < jnp.repeat(
        counts, tile_pairs
    )
    return jnp.where(live_rows[:, None], lagged, jnp.zeros_like(lagged))


def shards(windows, rotation, source_inverse, send_rows, tile_station, tile_count, pair_rows):
    ev_dev, components, stations, length = windows.shape
    half_len = length // 2
    owners = lax.axis_size("ev")
    dft_table = spectral_table(length)
    deconvolved = event_spectra(windows, rotation, source_inverse, dft_table)
    local_power = jnp.sum(
        deconvolved[..., :half_len] ** 2 + deconvolved[..., half_len:] ** 2, axis=0
    )
    power_sum = lax.psum(local_power, "ev")
    weight = 1.0 / (power_sum / (ev_dev * owners) + epsilon)
    capacity = send_rows.shape[1]
    slot_total = owners * capacity
    own_rows = deconvolved.astype(jnp.bfloat16).reshape(ev_dev * stations, length)
    received = lax.all_to_all(own_rows[send_rows], "ev", split_axis=0, concat_axis=0, tiled=True)
    received = received.reshape(slot_total, length)
    tiles_dev = tile_station.shape[0]
    tile_pairs = pair_rows.shape[1] // tiles_dev
    onehot = (tile_station[:, None] == jnp.arange(stations, dtype=jnp.int32)[None, :]).astype(
        jnp.float32
    )
    tile_weight = jnp.dot(onehot, weight, precision=lax.Precision.HIGHEST)
    groups = tiles_dev // 4
    group_rows = 4 * tile_pairs
    correlate = partial(correlate_group, received, lag_table(length, LAGS), tile_pairs)
    result = lax.map(
        correlate,
        (
            pair_rows[0].reshape(groups, group_rows),
            pair_rows[1].reshape(groups, group_rows),
            tile_weight.reshape(groups, 4, half_len),
            tile_count.reshape(groups, 4),
        ),
    )
    return result.reshape(groups * group_rows, LAGS)


def solution(mesh):
    in_specs = (
        P(("grp", "ev"), None, None, None),
        P(("grp", "ev"), None, None),
        P(("grp", "ev"), None),
        P(("grp", "ev"), None),
        P(("grp", "ev")),
        P(("grp", "ev")),
        P(None, ("grp", "ev")),
    )
    out_specs = P(("grp", "ev"), None)
    return jax.shard_map(shards, mesh=mesh, in_specs=in_specs, out_specs=out_specs, check_vma=False)
```

profile of v0, /device:TPU:0, one launch (start us, length us, event | category | flops | bytes accessed | tf_op | source)
XLA Modules:
  0.0 418.1 jit_solution(10348635386327450920)
XLA Ops:
  6.5 8.6 %multiply_convert_fusion = (bf16[1024,512]{1,0:T(8,128)(2,1)S(1)}, bf16[1024,512]{1,0:T(8,128)(2,1)S(1)}) fusion(), kind=kLoop, calls=%fused_computation.38 | loop fusion | flops 9961472 | bytes 2097152 | tf_op jit(solution)/shard_map/convert.10
  20.5 9.7 %gather_fusion.2 = bf16[2048,1024]{1,0:T(8,128)(2,1)} fusion(bf16[512,1024]{1,0:T(8,128)(2,1)S(1)} %pad_maximum_fusion, s32[2048]{0:T(1024)S(1)} %broadcast_clamp_fusion), kind=kCustom, calls=%fused_computation.2 | custom fusion | bytes 8396800 | tf_op jit(solution)/shard_map/gather | solution.py:89
  30.1 7.5 %all-to-all-start = ((bf16[32,64,1024]{2,1,0:T(8,128)(2,1)}), bf16[32,64,1024]{2,1,0:T(8,128)(2,1)}, u32[]{:S(2)}, u32[]{:S(2)}) async-start(bf16[32,64,1024]{2,1,0:T(8,128)(2,1)} %bitcast.58), calls=%async_computation | async-start | bytes 8388608 | tf_op jit(solution)/shard_map/all_to_all | solution.py:89
  41.8 148.0 %all-reduce.2.cloned.1.call-done = f32[64,512]{1,0:T(8,128)} async-done(((f32[64,512]{1,0:T(8,128)}), f32[64,512]{1,0:T(8,128)}) %all-reduce.2.cloned.1.call-update) | async-done | bytes 131088 | tf_op jit(solution)/shard_map/psum | solution.py:84
  191.1 220.2 %while.12 = (s32[]{:T(128)}, f32[16,512,255]{2,1,0:T(8,128)}, s32[16,4]{1,0:T(8,128)S(1)}, s32[16,512]{1,0:T(8,128)S(1)}, bf16[2048,1024]{1,0:T(8,128)(2,1)}, /*...) while((s32[]{:T(128)}, f32[16,512,255]{2,1,0:T(8,128)}, ...), condition=%wide.region_4.5_spmd, body=%wide.region_3.4_spmd.sunk | while | flops 273293312 | bytes 19963572 | solution.py:100
  191.1 5.5 %gather_fusion = bf16[512,1024]{1,0:T(8,128)(2,1)S(1)} fusion(bf16[2048,1024]{1,0:T(8,128)(2,1)} %get-tuple-element.218, s32[1024]{0:T(1024)S(1)} %pad_clamp_fusion.4), kind=kCustom, calls=%fused_computation.1.clone.1 | custom fusion | bytes 2099200 | tf_op jit(solution)/shard_map/while/body/eval_jaxpr/gather | solution.py:57
  196.8 5.5 %gather_fusion.1 = bf16[512,1024]{1,0:T(8,128)(2,1)S(1)} fusion(bf16[2048,1024]{1,0:T(8,128)(2,1)} %get-tuple-element.218, s32[1024]{0:T(1024)S(1)} %pad_clamp_fusion.5), kind=kCustom, calls=%fused_computation.clone.1 | custom fusion | bytes 2099200 | tf_op jit(solution)/shard_map/while/body/eval_jaxpr/gather | solution.py:56
  204.9 5.5 %gather_fusion = bf16[512,1024]{1,0:T(8,128)(2,1)S(1)} fusion(bf16[2048,1024]{1,0:T(8,128)(2,1)} %get-tuple-element.218, s32[1024]{0:T(1024)S(1)} %pad_clamp_fusion.4), kind=kCustom, calls=%fused_computation.1.clone.1 | custom fusion | bytes 2099200 | tf_op jit(solution)/shard_map/while/body/eval_jaxpr/gather | solution.py:57
  210.6 5.5 %gather_fusion.1 = bf16[512,1024]{1,0:T(8,128)(2,1)S(1)} fusion(bf16[2048,1024]{1,0:T(8,128)(2,1)} %get-tuple-element.218, s32[1024]{0:T(1024)S(1)} %pad_clamp_fusion.5), kind=kCustom, calls=%fused_computation.clone.1 | custom fusion | bytes 2099200 | tf_op jit(solution)/shard_map/while/body/eval_jaxpr/gather | solution.py:56
  218.6 5.5 %gather_fusion = bf16[512,1024]{1,0:T(8,128)(2,1)S(1)} fusion(bf16[2048,1024]{1,0:T(8,128)(2,1)} %get-tuple-element.218, s32[1024]{0:T(1024)S(1)} %pad_clamp_fusion.4), kind=kCustom, calls=%fused_computation.1.clone.1 | custom fusion | bytes 2099200 | tf_op jit(solution)/shard_map/while/body/eval_jaxpr/gather | solution.py:57
  224.4 5.5 %gather_fusion.1 = bf16[512,1024]{1,0:T(8,128)(2,1)S(1)} fusion(bf16[2048,1024]{1,0:T(8,128)(2,1)} %get-tuple-element.218, s32[1024]{0:T(1024)S(1)} %pad_clamp_fusion.5), kind=kCustom, calls=%fused_computation.clone.1 | custom fusion | bytes 2099200 | tf_op jit(solution)/shard_map/while/body/eval_jaxpr/gather | solution.py:56
  232.4 5.5 %gather_fusion = bf16[512,1024]{1,0:T(8,128)(2,1)S(1)} fusion(bf16[2048,1024]{1,0:T(8,128)(2,1)} %get-tuple-element.218, s32[1024]{0:T(1024)S(1)} %pad_clamp_fusion.4), kind=kCustom, calls=%fused_computation.1.clone.1 | custom fusion | bytes 2099200 | tf_op jit(solution)/shard_map/while/body/eval_jaxpr/gather | solution.py:57
  238.1 5.5 %gather_fusion.1 = bf16[512,1024]{1,0:T(8,128)(2,1)S(1)} fusion(bf16[2048,1024]{1,0:T(8,128)(2,1)} %get-tuple-element.218, s32[1024]{0:T(1024)S(1)} %pad_clamp_fusion.5), kind=kCustom, calls=%fused_computation.clone.1 | custom fusion | bytes 2099200 | tf_op jit(solution)/shard_map/while/body/eval_jaxpr/gather | solution.py:56
  259.9 5.5 %gather_fusion = bf16[512,1024]{1,0:T(8,128)(2,1)S(1)} fusion(bf16[2048,1024]{1,0:T(8,128)(2,1)} %get-tuple-element.218, s32[1024]{0:T(1024)S(1)} %pad_clamp_fusion.4), kind=kCustom, calls=%fused_computation.1.clone.1 | custom fusion | bytes 2099200 | tf_op jit(solution)/shard_map/while/body/eval_jaxpr/gather | solution.py:57
  265.6 5.5 %gather_fusion.1 = bf16[512,1024]{1,0:T(8,128)(2,1)S(1)} fusion(bf16[2048,1024]{1,0:T(8,128)(2,1)} %get-tuple-element.218, s32[1024]{0:T(1024)S(1)} %pad_clamp_fusion.5), kind=kCustom, calls=%fused_computation.clone.1 | custom fusion | bytes 2099200 | tf_op jit(solution)/shard_map/while/body/eval_jaxpr/gather | solution.py:56
  273.7 5.5 %gather_fusion = bf16[512,1024]{1,0:T(8,128)(2,1)S(1)} fusion(bf16[2048,1024]{1,0:T(8,128)(2,1)} %get-tuple-element.218, s32[1024]{0:T(1024)S(1)} %pad_clamp_fusion.4), kind=kCustom, calls=%fused_computation.1.clone.1 | custom fusion | bytes 2099200 | tf_op jit(solution)/shard_map/while/body/eval_jaxpr/gather | solution.py:57
  279.4 5.5 %gather_fusion.1 = bf16[512,1024]{1,0:T(8,128)(2,1)S(1)} fusion(bf16[2048,1024]{1,0:T(8,128)(2,1)} %get-tuple-element.218, s32[1024]{0:T(1024)S(1)} %pad_clamp_fusion.5), kind=kCustom, calls=%fused_computation.clone.1 | custom fusion | bytes 2099200 | tf_op jit(solution)/shard_map/while/body/eval_jaxpr/gather | solution.py:56
  287.4 5.5 %gather_fusion = bf16[512,1024]{1,0:T(8,128)(2,1)S(1)} fusion(bf16[2048,1024]{1,0:T(8,128)(2,1)} %get-tuple-element.218, s32[1024]{0:T(1024)S(1)} %pad_clamp_fusion.4), kind=kCustom, calls=%fused_computation.1.clone.1 | custom fusion | bytes 2099200 | tf_op jit(solution)/shard_map/while/body/eval_jaxpr/gather | solution.py:57
  293.2 5.5 %gather_fusion.1 = bf16[512,1024]{1,0:T(8,128)(2,1)S(1)} fusion(bf16[2048,1024]{1,0:T(8,128)(2,1)} %get-tuple-element.218, s32[1024]{0:T(1024)S(1)} %pad_clamp_fusion.5), kind=kCustom, calls=%fused_computation.clone.1 | custom fusion | bytes 2099200 | tf_op jit(solution)/shard_map/while/body/eval_jaxpr/gather | solution.py:56
  301.2 5.5 %gather_fusion = bf16[512,1024]{1,0:T(8,128)(2,1)S(1)} fusion(bf16[2048,1024]{1,0:T(8,128)(2,1)} %get-tuple-element.218, s32[1024]{0:T(1024)S(1)} %pad_clamp_fusion.4), kind=kCustom, calls=%fused_computation.1.clone.1 | custom fusion | bytes 2099200 | tf_op jit(solution)/shard_map/while/body/eval_jaxpr/gather | solution.py:57
  306.9 5.5 %gather_fusion.1 = bf16[512,1024]{1,0:T(8,128)(2,1)S(1)} fusion(bf16[2048,1024]{1,0:T(8,128)(2,1)} %get-tuple-element.218, s32[1024]{0:T(1024)S(1)} %pad_clamp_fusion.5), kind=kCustom, calls=%fused_computation.clone.1 | custom fusion | bytes 2099200 | tf_op jit(solution)/shard_map/while/body/eval_jaxpr/gather | solution.py:56
  315.0 5.5 %gather_fusion = bf16[512,1024]{1,0:T(8,128)(2,1)S(1)} fusion(bf16[2048,1024]{1,0:T(8,128)(2,1)} %get-tuple-element.218, s32[1024]{0:T(1024)S(1)} %pad_clamp_fusion.4), kind=kCustom, calls=%fused_computation.1.clone.1 | custom fusion | bytes 2099200 | tf_op jit(solution)/shard_map/while/body/eval_jaxpr/gather | solution.py:57
  320.7 5.5 %gather_fusion.1 = bf16[512,1024]{1,0:T(8,128)(2,1)S(1)} fusion(bf16[2048,1024]{1,0:T(8,128)(2,1)} %get-tuple-element.218, s32[1024]{0:T(1024)S(1)} %pad_clamp_fusion.5), kind=kCustom, calls=%fused_computation.clone.1 | custom fusion | bytes 2099200 | tf_op jit(solution)/shard_map/while/body/eval_jaxpr/gather | solution.py:56
  328.7 5.5 %gather_fusion = bf16[512,1024]{1,0:T(8,128)(2,1)S(1)} fusion(bf16[2048,1024]{1,0:T(8,128)(2,1)} %get-tuple-element.218, s32[1024]{0:T(1024)S(1)} %pad_clamp_fusion.4), kind=kCustom, calls=%fused_computation.1.clone.1 | custom fusion | bytes 2099200 | tf_op jit(solution)/shard_map/while/body/eval_jaxpr/gather | solution.py:57
  (240 shorter events, 125.9 us)
Async XLA Ops:
  6.5 8.6 %copy-start.4 = (bf16[8,3,64]{2,0,1:T(8,128)(2,1)S(1)}, bf16[8,3,64]{2,0,1:T(8,128)(2,1)}, u32[]{:S(2)}) copy-start(bf16[8,3,64]{2,0,1:T(8,128)(2,1)} %param.10) | copy-start | bytes 9220
  6.5 8.6 %copy-start.2 = (bf16[8,1024]{1,0:T(8,128)(2,1)S(1)}, bf16[8,1024]{1,0:T(8,128)(2,1)}, u32[]{:S(2)}) copy-start(bf16[8,1024]{1,0:T(8,128)(2,1)} %param.11) | copy-start | bytes 49156
  6.5 8.7 %copy-start.3 = (s32[32,64]{1,0:T(8,128)S(1)}, s32[32,64]{1,0:T(8,128)}, u32[]{:S(2)}) copy-start(s32[32,64]{1,0:T(8,128)} %param.12) | copy-start | bytes 24580
  30.1 8.2 %copy-start.1 = (s32[2,8192]{1,0:T(2,128)S(1)}, s32[2,8192]{1,0:T(2,128)}, u32[]{:S(2)}) copy-start(s32[2,8192]{1,0:T(2,128)} %param.15) | copy-start | bytes 196612
  30.1 8.4 %copy-start.5 = (s32[64]{0:T(128)S(1)}, s32[64]{0:T(128)}, u32[]{:S(2)}) copy-start(s32[64]{0:T(128)} %param.14) | copy-start | bytes 772
  30.1 159.7 %copy-start.6 = (s32[64]{0:T(128)S(1)}, s32[64]{0:T(128)}, u32[]{:S(2)}) copy-start(s32[64]{0:T(128)} %param.13) | copy-start | bytes 772
  30.1 160.9 %all-to-all-start = ((bf16[32,64,1024]{2,1,0:T(8,128)(2,1)}), bf16[32,64,1024]{2,1,0:T(8,128)(2,1)}, u32[]{:S(2)}, u32[]{:S(2)}) async-start(bf16[32,64,1024]{2,1,0:T(8,128)(2,1)} %bitcast.58), calls=%async_computation | async-start | bytes 8388608 | tf_op jit(solution)/shard_map/all_to_all | solution.py:89
  37.6 152.3 %all-reduce.2.cloned.1.call-start = ((), (), s32[]{:S(2)}) async-start(), calls=%async_computation.1 | async-start | bytes 262144 | tf_op jit(solution)/shard_map/psum | solution.py:84
  202.6 1.0 copy-start
  216.3 1.0 copy-start
  230.1 1.0 copy-start
  243.9 1.0 copy-start
  257.6 1.0 copy-start
  271.4 1.0 copy-start
  285.1 1.0 copy-start
  298.9 1.0 copy-start
  312.7 1.0 copy-start
  326.4 1.0 copy-start
  340.2 1.0 copy-start
  353.9 1.0 copy-start
  367.7 1.0 copy-start
  381.5 1.0 copy-start
  395.2 1.0 copy-start
  409.0 1.0 copy-start
Sparse Core Ops, SparseCore 0:
  43.9 145.8 all-reduce.1
where the time goes:
time: 420 us; the launch traced here: 418 us
  local copies, waits for them, and re-layouts  191 us (45%)
  waiting for transfers between devices  149 us (35%)
  other arithmetic  33.9 us (8%)
  matrix products  22.1 us (5%)
  between operations  13.6 us (3%)
  starting transfers between devices  7.5 us (2%)
    psum x1, waiting for transfers between devices, shards(): power_sum = lax.psum(local_power, 'ev')  148 us
    gather x16, local copies, waits for them, and re-layouts, correlate_group(): second_spec = spectra[second_rows].astype(jnp.float32)  87.3 us
    gather x16, local copies, waits for them, and re-layouts, correlate_group(): first_spec = spectra[first_rows].astype(jnp.float32)  87.3 us
    another operation x18, other arithmetic  19.9 us
    dot_general x16, matrix products, correlate_group(): lagged = jnp.dot(cross_spec, lag_tab, preferred_element_type=jnp.float32)  19.7 us
    gather x1, local copies, waits for them, and re-layouts, shards(): own_rows[send_rows]  9.66 us
  transfers between devices with their start and end apart: 2, of which 1 were waited for; matrix products, arithmetic and copies ran while one was open for 1% of the time, Pallas kernels for 0%

commit v1 on v0

--- a/solution.py
+++ b/solution.py
@@ -81,7 +81,7 @@
     local_power = jnp.sum(
         deconvolved[..., :half_len] ** 2 + deconvolved[..., half_len:] ** 2, axis=0
     )
-    power_sum = lax.psum(local_power, "ev")
+    power_sum = jnp.sum(lax.all_gather(local_power, "ev"), axis=0)
     weight = 1.0 / (power_sum / (ev_dev * owners) + epsilon)
     capacity = send_rows.shape[1]
     slot_total = owners * capacity

time: 420 us -> 378 us (0.900)
  waiting for transfers between devices: 149 us -> 105 us
    psum x1 -> x0, waiting for transfers between devices: 148 us -> none  [shards(): power_sum = lax.psum(local_power, 'ev')]
    all_gather x0 -> x1, waiting for transfers between devices: none -> 76.5 us  [shards(): power_sum = jnp.sum(lax.all_gather(local_power, 'ev'), axis=0)]
    all_to_all x1, waiting for transfers between devices: 0.01 us -> 28.6 us  [shards(): lax.all_to_all(own_rows[send_rows], 'ev', split_axis=0, concat_axis=0, ti...]
  transfers between devices with their start and end apart: 2 -> 2, of which waited for: 1 -> 2; matrix products, arithmetic and copies ran while one was open for 1% -> 4% of each run, Pallas kernels for 0% -> 0%
where the time goes in v1:
time: 378 us; the launch traced here: 376 us
  local copies, waits for them, and re-layouts  191 us (51%)
  waiting for transfers between devices  105 us (28%)
  other arithmetic  36.5 us (10%)
  matrix products  21.2 us (6%)
  between operations  13.6 us (4%)
  starting transfers between devices  7.46 us (2%)
    gather x16, local copies, waits for them, and re-layouts, correlate_group(): second_spec = spectra[second_rows].astype(jnp.float32)  87.3 us
    gather x16, local copies, waits for them, and re-layouts, correlate_group(): first_spec = spectra[first_rows].astype(jnp.float32)  87.3 us
    all_gather x1, waiting for transfers between devices, shards(): power_sum = jnp.sum(lax.all_gather(local_power, 'ev'), axis=0)  76.5 us
    all_to_all x1, waiting for transfers between devices, shards(): lax.all_to_all(own_rows[send_rows], 'ev', split_axis=0, concat_axis=0, ti...  28.6 us
    another operation x18, other arithmetic  19.9 us
    dot_general x16, matrix products, correlate_group(): lagged = jnp.dot(cross_spec, lag_tab, preferred_element_type=jnp.float32)  19.7 us
    gather x1, local copies, waits for them, and re-layouts, shards(): own_rows[send_rows]  9.63 us
  transfers between devices with their start and end apart: 2, of which 2 were waited for; matrix products, arithmetic and copies ran while one was open for 4% of the time, Pallas kernels for 0%

profile of v1, /device:TPU:0, one launch (start us, length us, event | category | flops | bytes accessed | tf_op | source)
XLA Modules:
  0.0 376.1 jit_solution(6486373038938365218)
XLA Ops:
  6.5 8.6 %multiply_convert_fusion = (bf16[1024,512]{1,0:T(8,128)(2,1)S(1)}, bf16[1024,512]{1,0:T(8,128)(2,1)S(1)}) fusion(), kind=kLoop, calls=%fused_computation.38 | loop fusion | flops 9961472 | bytes 2097152 | tf_op jit(solution)/shard_map/convert.10
  20.5 9.6 %gather_fusion.2 = bf16[2048,1024]{1,0:T(8,128)(2,1)} fusion(bf16[512,1024]{1,0:T(8,128)(2,1)S(1)} %pad_maximum_fusion, s32[2048]{0:T(1024)S(1)} %broadcast_clamp_fusion), kind=kCustom, calls=%fused_computation.2 | custom fusion | bytes 8396800 | tf_op jit(solution)/shard_map/gather | solution.py:89
  30.2 7.5 %all-to-all-start = ((bf16[32,64,1024]{2,1,0:T(8,128)(2,1)}), bf16[32,64,1024]{2,1,0:T(8,128)(2,1)}, u32[]{:S(2)}, u32[]{:S(2)}) async-start(bf16[32,64,1024]{2,1,0:T(8,128)(2,1)} %bitcast.59), calls=%async_computation | async-start | bytes 8388608 | tf_op jit(solution)/shard_map/all_to_all | solution.py:89
  41.1 76.5 %all-gather.3.cloned.1.call-done = f32[2048,512]{1,0:T(8,128)} async-done(((f32[64,512]{1,0:T(8,128)}), f32[2048,512]{1,0:T(8,128)}) %all-gather.3.cloned.1.call-update) | async-done | bytes 4194320 | tf_op jit(solution)/shard_map/all_gather | solution.py:84
  120.4 28.6 %all-to-all-done = bf16[32,64,1024]{2,1,0:T(8,128)(2,1)} async-done(((bf16[32,64,1024]{2,1,0:T(8,128)(2,1)}), bf16[32,64,1024]{2,1,0:T(8,128)(2,1)}, u32[]{:S(2)}, u32[]{:S(2)}) %all-to-all-start) | async-done | bytes 4194336 | tf_op jit(solution)/shard_map/all_to_all | solution.py:89
  149.0 220.2 %while.12 = (s32[]{:T(128)}, f32[16,512,255]{2,1,0:T(8,128)}, s32[16,4]{1,0:T(8,128)S(1)}, s32[16,512]{1,0:T(8,128)S(1)}, bf16[2048,1024]{1,0:T(8,128)(2,1)}, /*...) while((s32[]{:T(128)}, f32[16,512,255]{2,1,0:T(8,128)}, ...), condition=%wide.region_4.5_spmd, body=%wide.region_3.4_spmd.sunk | while | flops 273293312 | bytes 19963572 | solution.py:100
  149.1 5.5 %gather_fusion = bf16[512,1024]{1,0:T(8,128)(2,1)S(1)} fusion(bf16[2048,1024]{1,0:T(8,128)(2,1)} %get-tuple-element.218, s32[1024]{0:T(1024)S(1)} %pad_clamp_fusion.4), kind=kCustom, calls=%fused_computation.1.clone.1 | custom fusion | bytes 2099200 | tf_op jit(solution)/shard_map/while/body/eval_jaxpr/gather | solution.py:57
  154.8 5.5 %gather_fusion.1 = bf16[512,1024]{1,0:T(8,128)(2,1)S(1)} fusion(bf16[2048,1024]{1,0:T(8,128)(2,1)} %get-tuple-element.218, s32[1024]{0:T(1024)S(1)} %pad_clamp_fusion.5), kind=kCustom, calls=%fused_computation.clone.1 | custom fusion | bytes 2099200 | tf_op jit(solution)/shard_map/while/body/eval_jaxpr/gather | solution.py:56
  162.8 5.5 %gather_fusion = bf16[512,1024]{1,0:T(8,128)(2,1)S(1)} fusion(bf16[2048,1024]{1,0:T(8,128)(2,1)} %get-tuple-element.218, s32[1024]{0:T(1024)S(1)} %pad_clamp_fusion.4), kind=kCustom, calls=%fused_computation.1.clone.1 | custom fusion | bytes 2099200 | tf_op jit(solution)/shard_map/while/body/eval_jaxpr/gather | solution.py:57
  168.6 5.5 %gather_fusion.1 = bf16[512,1024]{1,0:T(8,128)(2,1)S(1)} fusion(bf16[2048,1024]{1,0:T(8,128)(2,1)} %get-tuple-element.218, s32[1024]{0:T(1024)S(1)} %pad_clamp_fusion.5), kind=kCustom, calls=%fused_computation.clone.1 | custom fusion | bytes 2099200 | tf_op jit(solution)/shard_map/while/body/eval_jaxpr/gather | solution.py:56
  176.6 5.5 %gather_fusion = bf16[512,1024]{1,0:T(8,128)(2,1)S(1)} fusion(bf16[2048,1024]{1,0:T(8,128)(2,1)} %get-tuple-element.218, s32[1024]{0:T(1024)S(1)} %pad_clamp_fusion.4), kind=kCustom, calls=%fused_computation.1.clone.1 | custom fusion | bytes 2099200 | tf_op jit(solution)/shard_map/while/body/eval_jaxpr/gather | solution.py:57
  182.3 5.5 %gather_fusion.1 = bf16[512,1024]{1,0:T(8,128)(2,1)S(1)} fusion(bf16[2048,1024]{1,0:T(8,128)(2,1)} %get-tuple-element.218, s32[1024]{0:T(1024)S(1)} %pad_clamp_fusion.5), kind=kCustom, calls=%fused_computation.clone.1 | custom fusion | bytes 2099200 | tf_op jit(solution)/shard_map/while/body/eval_jaxpr/gather | solution.py:56
  204.1 5.5 %gather_fusion = bf16[512,1024]{1,0:T(8,128)(2,1)S(1)} fusion(bf16[2048,1024]{1,0:T(8,128)(2,1)} %get-tuple-element.218, s32[1024]{0:T(1024)S(1)} %pad_clamp_fusion.4), kind=kCustom, calls=%fused_computation.1.clone.1 | custom fusion | bytes 2099200 | tf_op jit(solution)/shard_map/while/body/eval_jaxpr/gather | solution.py:57
  209.8 5.5 %gather_fusion.1 = bf16[512,1024]{1,0:T(8,128)(2,1)S(1)} fusion(bf16[2048,1024]{1,0:T(8,128)(2,1)} %get-tuple-element.218, s32[1024]{0:T(1024)S(1)} %pad_clamp_fusion.5), kind=kCustom, calls=%fused_computation.clone.1 | custom fusion | bytes 2099200 | tf_op jit(solution)/shard_map/while/body/eval_jaxpr/gather | solution.py:56
  217.9 5.5 %gather_fusion = bf16[512,1024]{1,0:T(8,128)(2,1)S(1)} fusion(bf16[2048,1024]{1,0:T(8,128)(2,1)} %get-tuple-element.218, s32[1024]{0:T(1024)S(1)} %pad_clamp_fusion.4), kind=kCustom, calls=%fused_computation.1.clone.1 | custom fusion | bytes 2099200 | tf_op jit(solution)/shard_map/while/body/eval_jaxpr/gather | solution.py:57
  223.6 5.5 %gather_fusion.1 = bf16[512,1024]{1,0:T(8,128)(2,1)S(1)} fusion(bf16[2048,1024]{1,0:T(8,128)(2,1)} %get-tuple-element.218, s32[1024]{0:T(1024)S(1)} %pad_clamp_fusion.5), kind=kCustom, calls=%fused_computation.clone.1 | custom fusion | bytes 2099200 | tf_op jit(solution)/shard_map/while/body/eval_jaxpr/gather | solution.py:56
  231.6 5.5 %gather_fusion = bf16[512,1024]{1,0:T(8,128)(2,1)S(1)} fusion(bf16[2048,1024]{1,0:T(8,128)(2,1)} %get-tuple-element.218, s32[1024]{0:T(1024)S(1)} %pad_clamp_fusion.4), kind=kCustom, calls=%fused_computation.1.clone.1 | custom fusion | bytes 2099200 | tf_op jit(solution)/shard_map/while/body/eval_jaxpr/gather | solution.py:57
  237.4 5.5 %gather_fusion.1 = bf16[512,1024]{1,0:T(8,128)(2,1)S(1)} fusion(bf16[2048,1024]{1,0:T(8,128)(2,1)} %get-tuple-element.218, s32[1024]{0:T(1024)S(1)} %pad_clamp_fusion.5), kind=kCustom, calls=%fused_computation.clone.1 | custom fusion | bytes 2099200 | tf_op jit(solution)/shard_map/while/body/eval_jaxpr/gather | solution.py:56
  259.2 5.5 %gather_fusion = bf16[512,1024]{1,0:T(8,128)(2,1)S(1)} fusion(bf16[2048,1024]{1,0:T(8,128)(2,1)} %get-tuple-element.218, s32[1024]{0:T(1024)S(1)} %pad_clamp_fusion.4), kind=kCustom, calls=%fused_computation.1.clone.1 | custom fusion | bytes 2099200 | tf_op jit(solution)/shard_map/while/body/eval_jaxpr/gather | solution.py:57
  264.9 5.5 %gather_fusion.1 = bf16[512,1024]{1,0:T(8,128)(2,1)S(1)} fusion(bf16[2048,1024]{1,0:T(8,128)(2,1)} %get-tuple-element.218, s32[1024]{0:T(1024)S(1)} %pad_clamp_fusion.5), kind=kCustom, calls=%fused_computation.clone.1 | custom fusion | bytes 2099200 | tf_op jit(solution)/shard_map/while/body/eval_jaxpr/gather | solution.py:56
  272.9 5.5 %gather_fusion = bf16[512,1024]{1,0:T(8,128)(2,1)S(1)} fusion(bf16[2048,1024]{1,0:T(8,128)(2,1)} %get-tuple-element.218, s32[1024]{0:T(1024)S(1)} %pad_clamp_fusion.4), kind=kCustom, calls=%fused_computation.1.clone.1 | custom fusion | bytes 2099200 | tf_op jit(solution)/shard_map/while/body/eval_jaxpr/gather | solution.py:57
  278.6 5.5 %gather_fusion.1 = bf16[512,1024]{1,0:T(8,128)(2,1)S(1)} fusion(bf16[2048,1024]{1,0:T(8,128)(2,1)} %get-tuple-element.218, s32[1024]{0:T(1024)S(1)} %pad_clamp_fusion.5), kind=kCustom, calls=%fused_computation.clone.1 | custom fusion | bytes 2099200 | tf_op jit(solution)/shard_map/while/body/eval_jaxpr/gather | solution.py:56
  286.7 5.5 %gather_fusion = bf16[512,1024]{1,0:T(8,128)(2,1)S(1)} fusion(bf16[2048,1024]{1,0:T(8,128)(2,1)} %get-tuple-element.218, s32[1024]{0:T(1024)S(1)} %pad_clamp_fusion.4), kind=kCustom, calls=%fused_computation.1.clone.1 | custom fusion | bytes 2099200 | tf_op jit(solution)/shard_map/while/body/eval_jaxpr/gather | solution.py:57
  292.4 5.5 %gather_fusion.1 = bf16[512,1024]{1,0:T(8,128)(2,1)S(1)} fusion(bf16[2048,1024]{1,0:T(8,128)(2,1)} %get-tuple-element.218, s32[1024]{0:T(1024)S(1)} %pad_clamp_fusion.5), kind=kCustom, calls=%fused_computation.clone.1 | custom fusion | bytes 2099200 | tf_op jit(solution)/shard_map/while/body/eval_jaxpr/gather | solution.py:56
  (241 shorter events, 132.3 us)
Async XLA Ops:
  6.5 8.6 %copy-start.4 = (bf16[8,3,64]{2,0,1:T(8,128)(2,1)S(1)}, bf16[8,3,64]{2,0,1:T(8,128)(2,1)}, u32[]{:S(2)}) copy-start(bf16[8,3,64]{2,0,1:T(8,128)(2,1)} %param.10) | copy-start | bytes 9220
  6.5 8.6 %copy-start.2 = (bf16[8,1024]{1,0:T(8,128)(2,1)S(1)}, bf16[8,1024]{1,0:T(8,128)(2,1)}, u32[]{:S(2)}) copy-start(bf16[8,1024]{1,0:T(8,128)(2,1)} %param.11) | copy-start | bytes 49156
  6.5 111.0 %all-gather.3.cloned.1.call-start = ((), (), s32[]{:S(2)}) async-start(), calls=%async_computation.1 | async-start | bytes 4325376 | tf_op jit(solution)/shard_map/all_gather | solution.py:84
  19.2 1.1 copy-start.3
  30.2 7.5 %copy-start.1 = (s32[2,8192]{1,0:T(2,128)S(1)}, s32[2,8192]{1,0:T(2,128)}, u32[]{:S(2)}) copy-start(s32[2,8192]{1,0:T(2,128)} %param.15) | copy-start | bytes 196612
  30.2 7.7 %copy-start.5 = (s32[64]{0:T(128)S(1)}, s32[64]{0:T(128)}, u32[]{:S(2)}) copy-start(s32[64]{0:T(128)} %param.14) | copy-start | bytes 772
  30.2 118.9 %all-to-all-start = ((bf16[32,64,1024]{2,1,0:T(8,128)(2,1)}), bf16[32,64,1024]{2,1,0:T(8,128)(2,1)}, u32[]{:S(2)}, u32[]{:S(2)}) async-start(bf16[32,64,1024]{2,1,0:T(8,128)(2,1)} %bitcast.59), calls=%async_computation | async-start | bytes 8388608 | tf_op jit(solution)/shard_map/all_to_all | solution.py:89
  117.6 2.5 copy-start.6
  160.5 1.0 copy-start
  174.3 1.0 copy-start
  188.1 1.0 copy-start
  201.8 1.0 copy-start
  215.6 1.0 copy-start
  229.3 1.0 copy-start
  243.1 1.0 copy-start
  256.9 1.0 copy-start
  270.6 1.0 copy-start
  284.4 1.0 copy-start
  298.1 1.0 copy-start
  311.9 1.0 copy-start
  325.7 1.0 copy-start
  339.4 1.0 copy-start
  353.2 1.0 copy-start
  366.9 1.0 copy-start
Sparse Core Ops, SparseCore 0:
  20.4 97.1 all-gather.2
